TPU v7x, 32 devices: a whole 2x2x4 slice. The times are simulated.
32 devices in a mesh: row: 8 (over y, x, core), col: 4 (over z).
Axes of the slice: x: 2, y: 2, z: 4, core: 2. Of those that a mesh axis runs over, the one named last changes fastest.
Arguments:
- trailing: float32 [512, 512], P('row', 'col'), may hold values from -6 to 6
- panel_block: bfloat16 [512, 1024], P('row'), may hold values from -24 to 24
- diag_inverse: bfloat16 [1024, 1024], P('col'), as said below
- panel_points: float32 [20, 1024], replicated, may hold values from 0 to 1
- lengthscales: float32 [20], replicated, may hold values from 0.15 to 5
- targets: bfloat16 [1024], replicated, may hold values from -96 to 96
- base_a: float32 [20, 24576], P(None, 'row'), may hold values from 0 to 1
- base_b: float32 [20, 24576], P(None, 'row'), may hold values from 0 to 1
- pick_sets: int32 [96, 20], P('row'), may hold values 0 or 1
- cross_rhs: bfloat16 [512, 24576], P('col', 'row'), may hold values from -0.59765625 to 0.59765625
- mean_in: float32 [24576], P('row'), may hold values from -3 to 3
- var_in: float32 [24576], P('row'), may hold values from 1 to 2
Outputs:
- trailing_next: float32 [512, 512], P('row', 'col')
- cross_next: bfloat16 [512, 24576], P('col', 'row')
- post_mean: float32 [24576], P('row')
- post_variance: float32 [24576], P('row')
Inputs may be any that keep to these rules, and one draw needn't show every extreme that they name: diag_inverse is lower triangular.
All inputs are finite; a program needn't handle non-finite values. No bound on the sum of `pick_sets` on one device may be relied on, other than what follows from the above.
Results may differ from a plain program's by a relative error of at most 0.0034.
Values may be sent and summed in bfloat16 or wider, within the bound.
No kernel may reach another device: no remote copies, remote signals or barrier semaphores. Data moves between devices by JAX's collectives and lax.ppermute only.
A program may use at most 64 MiB of HBM per device.

v0:
```python
import jax
import jax.numpy as jnp
from jax import lax
from jax.sharding import PartitionSpec as P

QB = 256


def kernel_block(scaled_points, candidates):
    inner = lax.dot_general(
        scaled_points,
        candidates,
        (((0,), (0,)), ((), ())),
        precision=lax.Precision.HIGHEST,
        preferred_element_type=jnp.float32,
    )
    distance = (
        jnp.sum(scaled_points * scaled_points, axis=0)[:, None]
        + jnp.sum(candidates * candidates, axis=0)[None, :]
        - 2.0 * inner
    )
    return jnp.exp(-0.5 * distance).astype(jnp.bfloat16)


def local(
    trailing,
    panel_block,
    diag_inverse,
    panel_points,
    lengthscales,
    targets,
    base_a,
    base_b,
    pick_sets,
    cross_rhs,
    mean_in,
    var_in,
):
    slab_cols = lax.dot_general(
        panel_block, diag_inverse, (((1,), (1,)), ((), ())), preferred_element_type=jnp.float32
    ).astype(jnp.bfloat16)
    own_rows = lax.all_gather(slab_cols, "col", axis=1, tiled=True)
    slice_height = own_rows.shape[0] // lax.axis_size("col")
    own_slice = lax.dynamic_slice_in_dim(
        own_rows, lax.axis_index("col") * slice_height, slice_height, 0
    )
    cyc_rows = lax.all_gather(own_slice, "row", axis=0, tiled=True)
    trailing_next = trailing - lax.dot_general(
        own_rows, cyc_rows, (((1,), (1,)), ((), ())), preferred_element_type=jnp.float32
    )
    chosen = jnp.repeat(pick_sets, QB, axis=0).T
    scaled_points = panel_points / lengthscales[:, None]
    candidates = jnp.where(chosen == 1, base_b, base_a) / lengthscales[:, None]
    kernel_cols = kernel_block(scaled_points, candidates)
    solve_slab = jnp.dot(diag_inverse, kernel_cols, preferred_element_type=jnp.float32).astype(
        jnp.bfloat16
    )
    weight_slab = jnp.dot(diag_inverse, targets, preferred_element_type=jnp.float32).astype(
        jnp.bfloat16
    )
    solve_piece = lax.all_gather(solve_slab, "col", axis=0, tiled=True)
    weight_piece = lax.all_gather(weight_slab, "col", axis=0, tiled=True)
    update_sum = jnp.dot(cyc_rows, solve_piece, preferred_element_type=jnp.float32)
    mean_sum = jnp.dot(weight_piece, solve_piece, preferred_element_type=jnp.float32)
    widened = solve_piece.astype(jnp.float32)
    square_sum = jnp.sum(widened * widened, axis=0)
    update_sum, mean_sum, square_sum = (update_sum, mean_sum, square_sum)
    cross_next = (cross_rhs.astype(jnp.float32) - update_sum).astype(jnp.bfloat16)
    post_mean = mean_in + mean_sum
    post_variance = var_in - square_sum
    return (trailing_next, cross_next, post_mean, post_variance)


def solution(mesh):
    placed = (
        P("row", "col"),
        P("row", None),
        P("col", None),
        P(),
        P(),
        P(),
        P(None, "row"),
        P(None, "row"),
        P("row", None),
        P("col", "row"),
        P("row"),
        P("row"),
    )
    return jax.shard_map(
        local,
        mesh=mesh,
        in_specs=placed,
        out_specs=(P("row", "col"), P("col", "row"), P("row"), P("row")),
        check_vma=False,
    )
```

profile of v0, /device:TPU:0, one launch (start us, length us, event | category | flops | bytes accessed | tf_op | source)
XLA Modules:
  0.0 166.4 jit_solution(10842736419029884639)
XLA Ops:
  7.2 0.0 copy-start
  7.2 0.0 all-gather.3.cloned.1.call-start
  7.2 0.8 broadcast_compare_fusion
  8.0 0.1 copy.18
  8.1 0.1 broadcast_bitcast_fusion
  8.3 1.0 multiply_reduce_fusion.2
  9.3 1.2 multiply_reduce_fusion.1
  10.5 14.2 %exponential_convert_fusion = bf16[1024,3072]{1,0:T(8,128)(2,1)S(1)} fusion(f32[3072]{0:T(1024)S(1)} %multiply_reduce_fusion.1, f32[1024]{0:T(1024)S(1)} %multiply_reduce_fusion.2, f32[20,1024]{1,0:T(8,128)} %param.15, f32[20]{0:T(128)} %param.16, f32[20,3072]{1,0:T(8,128)} %param.19, f32[20,3072]{1,0:T(8,128)} %param.18, pred[3072,20]{0,1:T(8,128)(4,1)S(1)} %bitcast.30), kind=kOutput, calls=%fused_computation.1 | convolution fusion | flops 770846720 | bytes 6942800 | tf_op jit(solution)/shard_map/dot_general | solution.py:10
  24.7 0.0 copy-done
  24.7 0.0 copy-start.7
  24.7 0.0 copy-start.3
  24.7 0.0 copy-start.4
  24.7 3.2 %fusion = bf16[256,3072]{0,1:T(8,128)(2,1)} fusion(bf16[1024,3072]{1,0:T(8,128)(2,1)S(1)} %exponential_convert_fusion, bf16[256,1024]{1,0:T(8,128)(2,1)S(1)} %copy-done), kind=kOutput, calls=%fused_computation.4 | convolution fusion | flops 1611399168 | bytes 8388608 | tf_op jit(solution)/shard_map/dot_general | solution.py:55
  27.9 0.0 copy-start.5
  27.9 0.0 all-gather.3.cloned.1.call-update
  27.9 0.0 copy-done.7
  28.0 0.2 fusion.2
  28.2 12.6 %all-gather = bf16[4,1,256]{2,1,0:T(2,128)(2,1)S(1)} all-gather(bf16[1,1,256]{2,1,0:T(2,128)(2,1)S(1)} %reshape.14), channel_id=1, replica_groups=mesh['row'=8,'col'=4] {'col'}, dimensions={0}, use_global_device_ids=true | all-gather | bytes 2560 | tf_op jit(solution)/shard_map/all_gather | solution.py:62
  40.8 0.0 copy-done.3
  40.8 0.3 convolution_convert_fusion.1
  41.1 38.7 %all_gather.12 = bf16[64,1024]{1,0:T(8,128)(2,1)S(1)} all-gather(bf16[64,256]{1,0:T(8,128)(2,1)S(1)} %convolution_convert_fusion.1), channel_id=1, replica_groups=mesh['row'=8,'col'=4] {'col'}, dimensions={1}, use_global_device_ids=true | all-gather | bytes 163840 | tf_op jit(solution)/shard_map/all_gather | solution.py:42
  79.8 9.5 %all_gather.13 = bf16[128,1024]{1,0:T(8,128)(2,1)S(1)} all-gather(bf16[16,1024]{1,0:T(8,128)(2,1)S(1)} %constant_dynamic-slice_fusion), channel_id=1, replica_groups=mesh['row'=8,'col'=4] {'row'}, dimensions={0}, use_global_device_ids=true | all-gather | bytes 294912 | tf_op jit(solution)/shard_map/all_gather | solution.py:47
  89.3 0.0 copy-done.4
  89.3 0.8 convolution_subtract_fusion.1
  90.1 59.2 %all-gather.3.cloned.1.call-done = bf16[1024,3072]{0,1:T(8,128)(2,1)} async-done(((bf16[256,3072]{0,1:T(8,128)(2,1)}), bf16[1024,3072]{0,1:T(8,128)(2,1)}) %all-gather.3.cloned.1.call-update) | async-done | bytes 6291472 | tf_op jit(solution)/shard_map/all_gather | solution.py:61
  149.3 0.0 copy-start.1
  149.3 0.0 copy-start.6
  149.3 0.0 copy-start.2
  149.3 4.7 %fusion.3 = f32[1,3072]{1,0:T(1,128)S(1)} fusion(bf16[1024,1]{0,1:T(2,128)(2,1)S(1)} %bitcast.32, bf16[1024,3072]{0,1:T(8,128)(2,1)} %all-gather.3.cloned.1.call-done), kind=kOutput, calls=%fused_computation.16 | convolution fusion | flops 6291456 | bytes 6305792 | tf_op jit(solution)/shard_map/dot_general | solution.py:64
  153.9 0.0 copy-done.5
  153.9 0.6 add.23
  154.6 0.0 copy-done.1
  154.6 1.3 multiply_reduce_fusion
  155.9 0.0 copy-done.6
  155.9 0.6 sub.15
  156.5 0.0 copy-done.2
  156.5 3.1 %fusion.1 = bf16[128,3072]{1,0:T(8,128)(2,1)} fusion(bf16[128,1024]{1,0:T(8,128)(2,1)S(1)} %all_gather.13, bf16[1024,3072]{0,1:T(8,128)(2,1)S(1)} %copy-done.1, bf16[128,3072]{1,0:T(8,128)(2,1)S(1)} %copy-done.2), kind=kOutput, calls=%fused_computation.5 | convolution fusion | flops 806486016 | bytes 8126464 | tf_op jit(solution)/shard_map/dot_general | solution.py:63
  (6 shorter events, 0.1 us)
Async XLA Ops:
  7.2 17.5 %copy-start = (bf16[256,1024]{1,0:T(8,128)(2,1)S(1)}, bf16[256,1024]{1,0:T(8,128)(2,1)}, u32[]{:S(2)}) copy-start(bf16[256,1024]{1,0:T(8,128)(2,1)} %param.14) | copy-start | bytes 1572868
  7.2 142.1 %all-gather.3.cloned.1.call-start = ((), (), s32[]{:S(2)}) async-start(), calls=%async_computation | async-start | bytes 7864320 | tf_op jit(solution)/shard_map/all_gather | solution.py:61
  24.7 3.2 %copy-start.7 = (bf16[1024]{0:T(1024)(128)(2,1)S(1)}, bf16[1024]{0:T(1024)(128)(2,1)}, u32[]{:S(2)}) copy-start(bf16[1024]{0:T(1024)(128)(2,1)} %param.17) | copy-start | bytes 6148
  24.7 16.1 %copy-start.3 = (bf16[64,1024]{1,0:T(8,128)(2,1)S(1)}, bf16[64,1024]{1,0:T(8,128)(2,1)}, u32[]{:S(2)}) copy-start(bf16[64,1024]{1,0:T(8,128)(2,1)} %param.13) | copy-start | bytes 393220
  24.7 64.5 %copy-start.4 = (f32[64,128]{1,0:T(8,128)S(1)}, f32[64,128]{1,0:T(8,128)}, u32[]{:S(2)}) copy-start(f32[64,128]{1,0:T(8,128)} %param.12) | copy-start | bytes 98308
  27.9 126.0 %copy-start.5 = (f32[3072]{0:T(1024)S(1)}, f32[3072]{0:T(1024)}, u32[]{:S(2)}) copy-start(f32[3072]{0:T(1024)} %param.22) | copy-start | bytes 36868
  149.3 5.3 %copy-start.1 = (bf16[1024,3072]{0,1:T(8,128)(2,1)S(1)}, bf16[1024,3072]{0,1:T(8,128)(2,1)}, u32[]{:S(2)}) copy-start(bf16[1024,3072]{0,1:T(8,128)(2,1)} %all-gather.3.cloned.1.call-done) | copy-start | bytes 18874372
  149.3 6.6 %copy-start.6 = (f32[3072]{0:T(1024)S(1)}, f32[3072]{0:T(1024)}, u32[]{:S(2)}) copy-start(f32[3072]{0:T(1024)} %param.23) | copy-start | bytes 36868
  149.3 7.2 %copy-start.2 = (bf16[128,3072]{1,0:T(8,128)(2,1)S(1)}, bf16[128,3072]{1,0:T(8,128)(2,1)}, u32[]{:S(2)}) copy-start(bf16[128,3072]{1,0:T(8,128)(2,1)} %param.21) | copy-start | bytes 2359300
Sparse Core Ops, SparseCore 0:
  28.0 121.1 all-gather.2
where the time goes:
time: 167 us; the launch traced here: 166 us
  blocking collectives  60.8 us (36%)
  waiting for transfers between devices  59.2 us (35%)
  matrix products  26.4 us (16%)
  between operations  14.2 us (9%)
  other arithmetic  5.48 us (3%)
    all_gather x1, waiting for transfers between devices, local(): solve_piece = lax.all_gather(solve_slab, 'col', axis=0, tiled=True)  59.2 us
    all_gather x1, blocking collectives, local(): own_rows = lax.all_gather(slab_cols, 'col', axis=1, tiled=True)  38.7 us
    dot_general x1, matrix products, kernel_block(): lax.dot_general(scaled_points, candidates, (((0,), (0,)), ((), ())), prec...  14.2 us
    all_gather x1, blocking collectives, local(): weight_piece = lax.all_gather(weight_slab, 'col', axis=0, tiled=True)  12.6 us
    all_gather x1, blocking collectives, local(): cyc_rows = lax.all_gather(own_slice, 'row', axis=0, tiled=True)  9.47 us
    dot_general x1, matrix products, local(): jnp.dot(weight_piece, solve_piece, preferred_element_type=jnp.float32)  4.65 us
  transfers between devices with their start and end apart: 1, of which 1 were waited for; matrix products, arithmetic and copies ran while one was open for 1% of the time, Pallas kernels for 0%

commit v1 on v0

--- a/solution.py
+++ b/solution.py
@@ -59,7 +59,12 @@
         jnp.bfloat16
     )
     solve_piece = lax.all_gather(solve_slab, "col", axis=0, tiled=True)
-    weight_piece = lax.all_gather(weight_slab, "col", axis=0, tiled=True)
+    ring = [weight_slab]
+    for hop in range(3):
+        ring.append(lax.ppermute(ring[-1], "col", [(dev, (dev + 1) % 4) for dev in range(4)]))
+    weight_piece = jnp.roll(
+        jnp.concatenate(ring[::-1], axis=0), (lax.axis_index("col") + 1) * ring[0].shape[0], axis=0
+    )
     update_sum = jnp.dot(cyc_rows, solve_piece, preferred_element_type=jnp.float32)
     mean_sum = jnp.dot(weight_piece, solve_piece, preferred_element_type=jnp.float32)
     widened = solve_piece.astype(jnp.float32)

time: 167 us -> 165 us (0.988)
  blocking collectives: 60.8 us -> 23.1 us
  waiting for transfers between devices: 59.2 us -> 77.6 us
  starting transfers between devices: 0.04 us -> 16.1 us
    all_gather x1, blocking collectives: 38.7 us -> 13.8 us  [local(): own_rows = lax.all_gather(slab_cols, 'col', axis=1, tiled=True)]
    ppermute x0 -> x3, starting transfers between devices: none -> 16.1 us  [local(): lax.ppermute(ring[-1], 'col', [(dev, (dev + 1) % 4) for dev in range(4)])]
    all_gather x1 -> x0, blocking collectives: 12.6 us -> none  [local(): weight_piece = lax.all_gather(weight_slab, 'col', axis=0, tiled=True)]
    all_gather x1, waiting for transfers between devices: 59.2 us -> 68.6 us  [local(): solve_piece = lax.all_gather(solve_slab, 'col', axis=0, tiled=True)]
    ppermute x0 -> x3, waiting for transfers between devices: none -> 8.95 us  [local(): lax.ppermute(ring[-1], 'col', [(dev, (dev + 1) % 4) for dev in range(4)])]
  transfers between devices with their start and end apart: 1 -> 4, of which waited for: 1 -> 3; matrix products, arithmetic and copies ran while one was open for 1% -> 2% of each run, Pallas kernels for 0% -> 0%
where the time goes in v1:
time: 165 us
  waiting for transfers between devices  77.6 us (47%)
  matrix products  26.4 us (16%)
  blocking collectives  23.1 us (14%)
  starting transfers between devices  16.1 us (10%)
  between operations  14.2 us (9%)
  other arithmetic  5.48 us (3%)
  local copies, waits for them, and re-layouts  2.01 us (1%)
    all_gather x1, waiting for transfers between devices, local(): solve_piece = lax.all_gather(solve_slab, 'col', axis=0, tiled=True)  68.6 us
    ppermute x3, starting transfers between devices, local(): lax.ppermute(ring[-1], 'col', [(dev, (dev + 1) % 4) for dev in range(4)])  16.1 us
    dot_general x1, matrix products, kernel_block(): lax.dot_general(scaled_points, candidates, (((0,), (0,)), ((), ())), prec...  14.2 us
    all_gather x1, blocking collectives, local(): own_rows = lax.all_gather(slab_cols, 'col', axis=1, tiled=True)  13.8 us
    all_gather x1, blocking collectives, local(): cyc_rows = lax.all_gather(own_slice, 'row', axis=0, tiled=True)  9.26 us
    ppermute x3, waiting for transfers between devices, local(): lax.ppermute(ring[-1], 'col', [(dev, (dev + 1) % 4) for dev in range(4)])  8.95 us
    dot_general x1, matrix products, local(): jnp.dot(weight_piece, solve_piece, preferred_element_type=jnp.float32)  4.65 us
  transfers between devices with their start and end apart: 4, of which 3 were waited for; matrix products, arithmetic and copies ran while one was open for 2% of the time, Pallas kernels for 0%

profile of v1, /device:TPU:0, one launch (start us, length us, event | category | flops | bytes accessed | tf_op | source)
XLA Modules:
  0.0 164.8 jit_solution(2560468676040322787)
XLA Ops:
  7.2 0.0 copy-start
  7.2 0.0 all-gather.2.cloned.1.call-start
  7.2 0.8 broadcast_compare_fusion
  8.0 0.1 copy.17
  8.1 0.1 broadcast_bitcast_fusion
  8.3 1.0 multiply_reduce_fusion.2
  9.3 1.2 multiply_reduce_fusion.1
  10.5 14.2 %exponential_convert_fusion = bf16[1024,3072]{1,0:T(8,128)(2,1)S(1)} fusion(f32[3072]{0:T(1024)S(1)} %multiply_reduce_fusion.1, f32[1024]{0:T(1024)S(1)} %multiply_reduce_fusion.2, f32[20,1024]{1,0:T(8,128)} %param.15, f32[20]{0:T(128)} %param.16, f32[20,3072]{1,0:T(8,128)} %param.19, f32[20,3072]{1,0:T(8,128)} %param.18, pred[3072,20]{0,1:T(8,128)(4,1)S(1)} %bitcast.29), kind=kOutput, calls=%fused_computation.1 | convolution fusion | flops 770846720 | bytes 6942800 | tf_op jit(solution)/shard_map/dot_general | solution.py:10
  24.7 0.0 copy-done
  24.7 0.0 copy-start.7
  24.7 0.0 copy-start.3
  24.7 0.0 copy-start.4
  24.7 3.2 %fusion = bf16[256,3072]{0,1:T(8,128)(2,1)} fusion(bf16[1024,3072]{1,0:T(8,128)(2,1)S(1)} %exponential_convert_fusion, bf16[256,1024]{1,0:T(8,128)(2,1)S(1)} %copy-done), kind=kOutput, calls=%fused_computation.4 | convolution fusion | flops 1611399168 | bytes 8388608 | tf_op jit(solution)/shard_map/dot_general | solution.py:55
  27.9 0.0 copy-start.5
  27.9 0.0 all-gather.2.cloned.1.call-update
  27.9 0.0 copy-done.7
  28.0 0.2 fusion.2
  28.2 3.0 %collective-permute-start = (bf16[256]{0:T(256)(128)(2,1)S(1)}, bf16[256]{0:T(256)(128)(2,1)S(1)}, u32[]{:S(2)}, u32[]{:S(2)}) collective-permute-start(bf16[256]{0:T(256)(128)(2,1)S(1)} %convert_element_type.30), channel_id=1, source_target_pairs={{0,1},{1,2},{2,3},{3,0},{4,5},{5,6},{6,7},{7,4},{8,9},{9,10},{10,1... | collective-permute-start | bytes 1544 | tf_op jit(solution)/shard_map/ppermute | solution.py:64
  31.2 0.0 copy-done.3
  31.2 0.3 convolution_convert_fusion.1
  31.5 13.8 %all_gather.9 = bf16[64,1024]{1,0:T(8,128)(2,1)S(1)} all-gather(bf16[64,256]{1,0:T(8,128)(2,1)S(1)} %convolution_convert_fusion.1), channel_id=1, replica_groups=mesh['row'=8,'col'=4] {'col'}, dimensions={1}, use_global_device_ids=true | all-gather | bytes 163840 | tf_op jit(solution)/shard_map/all_gather | solution.py:42
  45.3 9.3 %all_gather.10 = bf16[128,1024]{1,0:T(8,128)(2,1)S(1)} all-gather(bf16[16,1024]{1,0:T(8,128)(2,1)S(1)} %constant_dynamic-slice_fusion), channel_id=1, replica_groups=mesh['row'=8,'col'=4] {'row'}, dimensions={0}, use_global_device_ids=true | all-gather | bytes 294912 | tf_op jit(solution)/shard_map/all_gather | solution.py:47
  54.6 0.0 copy-done.4
  54.6 0.8 convolution_subtract_fusion.1
  55.4 0.0 collective-permute-done
  55.4 0.6 collective-permute-start.1
  56.0 4.7 %collective-permute-done.1 = bf16[256]{0:T(256)(128)(2,1)S(1)} collective-permute-done((bf16[256]{0:T(256)(128)(2,1)S(1)}, bf16[256]{0:T(256)(128)(2,1)S(1)}, u32[]{:S(2)}, u32[]{:S(2)}) %collective-permute-start.1) | collective-permute-done | bytes 544 | tf_op jit(solution)/shard_map/ppermute | solution.py:64
  60.8 12.5 %collective-permute-start.2 = (bf16[256]{0:T(256)(128)(2,1)S(1)}, bf16[256]{0:T(256)(128)(2,1)S(1)}, u32[]{:S(2)}, u32[]{:S(2)}) collective-permute-start(bf16[256]{0:T(256)(128)(2,1)S(1)} %collective-permute-done.1), channel_id=1, source_target_pairs={{0,1},{1,2},{2,3},{3,0},{4,5},{5,6},{6,7},{7,4},{8,9},{9,10},{10,1... | collective-permute-start | bytes 1544 | tf_op jit(solution)/shard_map/ppermute | solution.py:64
  73.3 4.2 %collective-permute-done.2 = bf16[256]{0:T(256)(128)(2,1)S(1)} collective-permute-done((bf16[256]{0:T(256)(128)(2,1)S(1)}, bf16[256]{0:T(256)(128)(2,1)S(1)}, u32[]{:S(2)}, u32[]{:S(2)}) %collective-permute-start.2) | collective-permute-done | bytes 544 | tf_op jit(solution)/shard_map/ppermute | solution.py:64
  77.5 0.2 dynamic-update-slice
  77.6 0.2 dynamic-update-slice.1
  77.9 0.2 dynamic-update-slice.2
  78.1 0.2 dynamic-update-slice.3
  78.3 0.2 dynamic-update-slice.4
  78.5 0.2 dynamic-update-slice.5
  78.7 0.2 dynamic-update-slice.6
  78.8 0.2 dynamic-update-slice.7
  79.0 0.1 dynamic_slice.8
  79.1 0.0 copy-start.6
  79.1 68.6 %all-gather.2.cloned.1.call-done = bf16[1024,3072]{0,1:T(8,128)(2,1)} async-done(((bf16[256,3072]{0,1:T(8,128)(2,1)}), bf16[1024,3072]{0,1:T(8,128)(2,1)}) %all-gather.2.cloned.1.call-update) | async-done | bytes 6291472 | tf_op jit(solution)/shard_map/all_gather | solution.py:61
  147.7 0.0 copy-start.1
  147.7 0.0 copy-start.2
  147.7 4.7 %fusion.3 = f32[1,3072]{1,0:T(1,128)S(1)} fusion(bf16[1024,1]{0,1:T(2,128)(2,1)S(1)} %reshape.16, bf16[1024,3072]{0,1:T(8,128)(2,1)} %all-gather.2.cloned.1.call-done), kind=kOutput, calls=%fused_computation.16 | convolution fusion | flops 6291456 | bytes 6305792 | tf_op jit(solution)/shard_map/dot_general | solution.py:69
  152.4 0.0 copy-done.5
  152.4 0.6 add.39
  153.0 0.0 copy-done.1
  153.0 1.3 multiply_reduce_fusion
  154.3 0.0 copy-done.6
  154.3 0.6 sub.20
  154.9 0.0 copy-done.2
  154.9 3.1 %fusion.1 = bf16[128,3072]{1,0:T(8,128)(2,1)} fusion(bf16[128,1024]{1,0:T(8,128)(2,1)S(1)} %all_gather.10, bf16[1024,3072]{0,1:T(8,128)(2,1)S(1)} %copy-done.1, bf16[128,3072]{1,0:T(8,128)(2,1)S(1)} %copy-done.2), kind=kOutput, calls=%fused_computation.5 | convolution fusion | flops 806486016 | bytes 8126464 | tf_op jit(solution)/shard_map/dot_general | solution.py:68
  (7 shorter events, 0.1 us)
Async XLA Ops:
  7.2 17.5 %copy-start = (bf16[256,1024]{1,0:T(8,128)(2,1)S(1)}, bf16[256,1024]{1,0:T(8,128)(2,1)}, u32[]{:S(2)}) copy-start(bf16[256,1024]{1,0:T(8,128)(2,1)} %param.14) | copy-start | bytes 1572868
  7.2 140.5 %all-gather.2.cloned.1.call-start = ((), (), s32[]{:S(2)}) async-start(), calls=%async_computation | async-start | bytes 7864320 | tf_op jit(solution)/shard_map/all_gather | solution.py:61
  24.7 3.2 %copy-start.7 = (bf16[1024]{0:T(1024)(128)(2,1)S(1)}, bf16[1024]{0:T(1024)(128)(2,1)}, u32[]{:S(2)}) copy-start(bf16[1024]{0:T(1024)(128)(2,1)} %param.17) | copy-start | bytes 6148
  24.7 6.5 %copy-start.3 = (bf16[64,1024]{1,0:T(8,128)(2,1)S(1)}, bf16[64,1024]{1,0:T(8,128)(2,1)}, u32[]{:S(2)}) copy-start(bf16[64,1024]{1,0:T(8,128)(2,1)} %param.13) | copy-start | bytes 393220
  24.7 29.9 %copy-start.4 = (f32[64,128]{1,0:T(8,128)S(1)}, f32[64,128]{1,0:T(8,128)}, u32[]{:S(2)}) copy-start(f32[64,128]{1,0:T(8,128)} %param.12) | copy-start | bytes 98308
  27.9 124.5 %copy-start.5 = (f32[3072]{0:T(1024)S(1)}, f32[3072]{0:T(1024)}, u32[]{:S(2)}) copy-start(f32[3072]{0:T(1024)} %param.22) | copy-start | bytes 36868
  28.2 27.2 %collective-permute-start = (bf16[256]{0:T(256)(128)(2,1)S(1)}, bf16[256]{0:T(256)(128)(2,1)S(1)}, u32[]{:S(2)}, u32[]{:S(2)}) collective-permute-start(bf16[256]{0:T(256)(128)(2,1)S(1)} %convert_element_type.30), channel_id=1, source_target_pairs={{0,1},{1,2},{2,3},{3,0},{4,5},{5,6},{6,7},{7,4},{8,9},{9,10},{10,1... | collective-permute-start | bytes 1544 | tf_op jit(solution)/shard_map/ppermute | solution.py:64
  55.4 5.3 %collective-permute-start.1 = (bf16[256]{0:T(256)(128)(2,1)S(1)}, bf16[256]{0:T(256)(128)(2,1)S(1)}, u32[]{:S(2)}, u32[]{:S(2)}) collective-permute-start(bf16[256]{0:T(256)(128)(2,1)S(1)} %collective-permute-done), channel_id=1, source_target_pairs={{0,1},{1,2},{2,3},{3,0},{4,5},{5,6},{6,7},{7,4},{8,9},{9,10},{10,1... | collective-permute-start | bytes 1544 | tf_op jit(solution)/shard_map/ppermute | solution.py:64
  60.8 16.7 %collective-permute-start.2 = (bf16[256]{0:T(256)(128)(2,1)S(1)}, bf16[256]{0:T(256)(128)(2,1)S(1)}, u32[]{:S(2)}, u32[]{:S(2)}) collective-permute-start(bf16[256]{0:T(256)(128)(2,1)S(1)} %collective-permute-done.1), channel_id=1, source_target_pairs={{0,1},{1,2},{2,3},{3,0},{4,5},{5,6},{6,7},{7,4},{8,9},{9,10},{10,1... | collective-permute-start | bytes 1544 | tf_op jit(solution)/shard_map/ppermute | solution.py:64
  79.1 75.2 %copy-start.6 = (f32[3072]{0:T(1024)S(1)}, f32[3072]{0:T(1024)}, u32[]{:S(2)}) copy-start(f32[3072]{0:T(1024)} %param.23) | copy-start | bytes 36868
  147.7 5.3 %copy-start.1 = (bf16[1024,3072]{0,1:T(8,128)(2,1)S(1)}, bf16[1024,3072]{0,1:T(8,128)(2,1)}, u32[]{:S(2)}) copy-start(bf16[1024,3072]{0,1:T(8,128)(2,1)} %all-gather.2.cloned.1.call-done) | copy-start | bytes 18874372
  147.7 7.2 %copy-start.2 = (bf16[128,3072]{1,0:T(8,128)(2,1)S(1)}, bf16[128,3072]{1,0:T(8,128)(2,1)}, u32[]{:S(2)}) copy-start(bf16[128,3072]{1,0:T(8,128)(2,1)} %param.21) | copy-start | bytes 2359300
Sparse Core Ops, SparseCore 0:
  28.0 119.6 all-gather.1
